TPU v7x, 512 devices: a whole 4x4x16 slice. The times are simulated.
512 devices in a mesh: seq: 32 (over z_hi, x, core), sub: 16 (over z_lo, y).
Axes of the slice: x: 4, y: 4, z: 16 (z_hi: 4, z_lo: 4; z = z_hi * 4 + z_lo), core: 2. Of those that a mesh axis runs over, the one named last changes fastest.
Arguments:
- activations: bfloat16 [65536, 1024], P(('seq', 'sub')), may hold values from -6 to 6
- conv_weight: bfloat16 [5, 1152, 1024], P(None, 'sub'), may hold values from -1 to 1
- cotangent: bfloat16 [16384, 1152], P('seq', 'sub'), may hold values from -6 to 6
Outputs:
- features: bfloat16 [16384, 1152], P('seq', 'sub')
- input_grad: bfloat16 [65536, 1024], P(('seq', 'sub'))
- weight_grad: float32 [1024, 5, 1152], P('seq', None, 'sub')
All inputs are finite; a program needn't handle non-finite values.
Results may differ from a plain program's by a relative error of at most 0.02.
Values may be sent and summed in bfloat16 or wider, within the bound.
No kernel may reach another device: no remote copies, remote signals or barrier semaphores. Data moves between devices by JAX's collectives and lax.ppermute only.
A program may use at most 64 MiB of HBM per device.

v0:
```python
import jax
import jax.numpy as jnp
from jax import lax
from jax.sharding import PartitionSpec as P

EPSILON = 1e-06


def padded_2(block, sides, width):
    for axis, dim in sides:
        count = lax.axis_size(axis)
        forward = [(i, i + 1) for i in range(count - 1)]
        backward = [(target, source) for source, target in forward]
        low = lax.ppermute(
            lax.slice_in_dim(block, block.shape[dim] - width, None, axis=dim), axis, forward
        )
        high = lax.ppermute(lax.slice_in_dim(block, 0, width, axis=dim), axis, backward)
        block = jnp.concatenate([low, block, high], axis=dim)
    return block


def gelu_slope(tensor):
    return (
        0.5 * (1.0 + jax.scipy.special.erf(tensor * 0.7071067811865476))
        + tensor * jnp.exp(-0.5 * tensor * tensor) * 0.3989422804014327
    )


def pool_pairs(tensor):
    half_rows = tensor.shape[0] // 2
    return 0.5 * jnp.sum(tensor.reshape(half_rows, 2, tensor.shape[1]), axis=1)


def per_device(activations, conv_weight, cotangent):
    tap_count = conv_weight.shape[0]
    in_width = activations.shape[1]
    out_width = conv_weight.shape[1]
    full_out = out_width * lax.axis_size("sub")
    x_float = activations.astype(jnp.float32)
    inv_first = lax.rsqrt(jnp.mean(x_float * x_float, axis=1, keepdims=True) + EPSILON)
    normed_first = x_float * inv_first
    pooled = pool_pairs(jax.nn.gelu(normed_first, approximate=False)).astype(jnp.bfloat16)
    gathered = lax.all_gather(pooled, "sub", axis=0, tiled=True)
    block_rows = gathered.shape[0]
    padded = padded_2(gathered, (("seq", 0),), 2)
    conv_acc = jnp.zeros((block_rows, out_width), jnp.float32)
    for offset in range(tap_count):
        conv_acc = conv_acc + lax.dot_general(
            padded[offset : offset + block_rows],
            conv_weight[offset],
            (((1,), (1,)), ((), ())),
            preferred_element_type=jnp.float32,
        )
    conv_out = conv_acc.astype(jnp.bfloat16)
    y_float = conv_out.astype(jnp.float32)
    square_sum = lax.psum(jnp.sum(y_float * y_float, axis=1), "sub")
    inv_second = lax.rsqrt(square_sum / full_out + EPSILON)[:, None]
    normed_second = y_float * inv_second
    features = pool_pairs(jax.nn.gelu(normed_second, approximate=False)).astype(jnp.bfloat16)
    upstream = 0.5 * jnp.repeat(cotangent.astype(jnp.float32), 2, axis=0)
    slope_second = upstream * gelu_slope(normed_second)
    inner_second = lax.psum(jnp.sum(slope_second * normed_second, axis=1), "sub")
    conv_grad = (
        inv_second * (slope_second - normed_second * (inner_second / full_out)[:, None])
    ).astype(jnp.bfloat16)
    grad_padded = padded_2(conv_grad, (("seq", 0),), 2)
    running = jnp.zeros((block_rows, in_width), jnp.float32)
    for offset in range(tap_count):
        window = lax.dynamic_slice_in_dim(grad_padded, 0 + 4 - offset, block_rows, 0)
        running = running + jnp.dot(window, conv_weight[offset], preferred_element_type=jnp.float32)
    owned = lax.psum_scatter(
        running.astype(jnp.bfloat16), "sub", scatter_dimension=1, tiled=True
    ).astype(jnp.float32)
    pooled_grad = lax.all_to_all(
        owned.astype(jnp.bfloat16), "sub", split_axis=0, concat_axis=1, tiled=True
    ).astype(owned.dtype)
    slope_first = 0.5 * jnp.repeat(pooled_grad, 2, axis=0) * gelu_slope(normed_first)
    inner_first = jnp.mean(slope_first * normed_first, axis=1, keepdims=True)
    input_grad = (inv_first * (slope_first - normed_first * inner_first)).astype(jnp.bfloat16)
    pieces = [
        lax.dot_general(
            padded[offset : offset + block_rows],
            conv_grad,
            (((0,), (0,)), ((), ())),
            preferred_element_type=jnp.float32,
        )
        for offset in range(tap_count)
    ]
    weight_grad = lax.psum_scatter(
        jnp.stack(pieces, axis=1).astype(jnp.bfloat16), "seq", scatter_dimension=0, tiled=True
    ).astype(jnp.float32)
    return (features, input_grad, weight_grad)


def solution(mesh):
    return jax.shard_map(
        per_device,
        mesh=mesh,
        in_specs=(P(("seq", "sub"), None), P(None, "sub", None), P("seq", "sub")),
        out_specs=(P("seq", "sub"), P(("seq", "sub"), None), P("seq", None, "sub")),
        check_vma=False,
    )
```

profile of v0, /device:TPU:8, one launch (start us, length us, event | category | flops | bytes accessed | tf_op | source)
XLA Modules:
  0.0 446.3 jit_solution(8332122157335202841)
XLA Ops:
  7.2 1.1 fusion.93
  8.3 2.2 fusion.55
  10.5 0.3 reshape.38
  10.8 0.6 reduce_sum.55
  11.4 0.7 multiply_convert_fusion.2
  12.3 0.2 broadcast_in_dim.4
  12.7 91.6 %all-gather.2.cloned.1.call-done = bf16[1024,1024]{1,0:T(8,128)(2,1)} async-done(((bf16[64,1024]{1,0:T(8,128)(2,1)}), bf16[1024,1024]{1,0:T(8,128)(2,1)}) %all-gather.2.cloned.1.call-update) | async-done | bytes 2097168 | tf_op jit(solution)/shard_map/all_gather | solution.py:43
  104.3 0.9 fusion.151
  105.2 1.3 collective-permute-start
  106.5 1.3 collective-permute-start.1
  107.8 2.4 fusion.125
  110.3 0.9 collective-permute-done.1
  111.3 0.8 fusion.3
  112.1 0.7 fusion.9
  112.8 0.8 fusion.17
  113.6 1.7 multiply_reduce_fusion.1
  115.3 38.7 %psum.14 = f32[1024]{0:T(1024)S(1)} all-reduce(f32[1024]{0:T(1024)S(1)} %get-tuple-element.22), channel_id=1, replica_groups=mesh['seq'=32,'sub'=16] {'sub'}, use_global_device_ids=true, to_apply=%region_3.0 | all-reduce | flops 1024 | bytes 8192 | tf_op jit(solution)/shard_map/psum | solution.py:56
  154.2 42.8 %psum.15 = f32[1024]{0:T(1024)S(1)} all-reduce(f32[1024]{0:T(1024)S(1)} %get-tuple-element.14), channel_id=1, replica_groups=mesh['seq'=32,'sub'=16] {'sub'}, use_global_device_ids=true, to_apply=%region_6.0 | all-reduce | flops 1024 | bytes 8192 | tf_op jit(solution)/shard_map/psum | solution.py:62
  197.0 0.7 multiply_convert_fusion
  197.8 1.4 collective-permute-start.2
  199.2 1.7 fusion.123
  200.8 3.0 collective-permute-start.3
  203.9 0.8 fusion.117
  204.7 0.8 fusion.113
  205.5 0.8 fusion.110
  206.3 2.8 add_convert_fusion
  209.1 0.2 reduce-scatter.5.cloned.1.call-start
  209.4 0.7 fusion.32
  210.0 0.7 fusion.48
  210.7 0.5 fusion.34
  211.2 1.1 copy-done.3
  212.3 0.7 fusion.44
  213.0 0.7 fusion.38
  213.6 2.5 copy.17
  216.2 92.8 %reduce-scatter.3.cloned.1.call-done = bf16[1024,64]{0,1:T(8,128)(2,1)} async-done(((bf16[1024,1024]{0,1:T(8,128)(2,1)}), bf16[1024,64]{0,1:T(8,128)(2,1)}) %reduce-scatter.3.cloned.1.call-update) | async-done | bytes 131088 | tf_op jit(solution)/shard_map/reduce_scatter | solution.py:71
  308.9 1.1 copy.20
  310.0 0.9 reshape.40
  310.9 8.1 %all-to-all-start = ((bf16[16,2,2048]{2,1,0:T(2,128)(2,1)}), bf16[16,2,2048]{2,1,0:T(2,128)(2,1)S(1)}, u32[]{:S(2)}, u32[]{:S(2)}) async-start(bf16[16,2,2048]{2,1,0:T(2,128)(2,1)} %reshape.40), calls=%async_computation.1 | async-start | bytes 262144 | tf_op jit(solution)/shard_map/all_to_all | solution.py:74
  319.0 0.2 copy.12
  319.2 0.6 reduce_sum.57
  319.9 0.7 copy.18
  320.6 114.9 %reduce-scatter.5.cloned.1.call-done = bf16[32,5,72]{2,1,0:T(8,128)(2,1)} async-done(((bf16[1024,5,72]{2,1,0:T(8,128)(2,1)}), bf16[32,5,72]{2,1,0:T(8,128)(2,1)}) %reduce-scatter.5.cloned.1.call-update) | async-done | bytes 23056 | tf_op jit(solution)/shard_map/reduce_scatter | solution.py:89
  435.5 1.5 copy.19
  437.0 0.2 reshape.41
  437.3 0.3 copy.16
  438.0 0.4 mul.194
  438.4 0.4 fusion.92
  438.8 1.0 fusion.90
  (37 shorter events, 1.4 us)
Async XLA Ops:
  7.2 5.0 %copy-start.6 = (bf16[512,72]{0,1:T(8,128)(2,1)S(1)}, bf16[512,72]{0,1:T(8,128)(2,1)}, u32[]{:S(2)}) copy-start(bf16[512,72]{0,1:T(8,128)(2,1)} %param.5) | copy-start | bytes 221188
  7.2 97.1 %all-gather.2.cloned.1.call-start = ((), (), s32[]{:S(2)}) async-start(), calls=%async_computation.3 | async-start | bytes 2228224 | tf_op jit(solution)/shard_map/all_gather | solution.py:43
  10.5 97.3 %copy-start.4 = (bf16[5,72,1024]{2,1,0:T(8,128)(2,1)S(1)}, bf16[5,72,1024]{2,1,0:T(8,128)(2,1)}, u32[]{:S(2)}) copy-start(bf16[5,72,1024]{2,1,0:T(8,128)(2,1)} %param.4) | copy-start | bytes 2211844
  12.1 296.8 %reduce-scatter.3.cloned.1.call-start = ((), (), s32[]{:S(2)}) async-start(), calls=%async_computation.4 | async-start | bytes 2228224 | tf_op jit(solution)/shard_map/reduce_scatter | solution.py:71
  104.3 5.9 %copy-start = (bf16[1024,1024]{1,0:T(8,128)(2,1)S(1)}, bf16[1024,1024]{1,0:T(8,128)(2,1)}, u32[]{:S(2)}) copy-start(bf16[1024,1024]{1,0:T(8,128)(2,1)} %all-gather.2.cloned.1.call-done) | copy-start | bytes 6291460
  105.2 6.8 %collective-permute-start = (bf16[2,1024]{1,0:T(2,128)(2,1)S(1)}, bf16[2,1024]{1,0:T(2,128)(2,1)S(1)}, u32[]{:S(2)}, u32[]{:S(2)}) collective-permute-start(bf16[2,1024]{1,0:T(2,128)(2,1)S(1)} %get-tuple-element.16), channel_id=1, source_target_pairs={{0,16},{16,32},{32,48},{48,64},{64,80},{80,96},{96,112},{112,128},... | collective-permute-start | bytes 12296 | tf_op jit(solution)/shard_map/ppermute | solution.py:14
  106.5 4.8 %collective-permute-start.1 = (bf16[2,1024]{1,0:T(2,128)(2,1)S(1)}, bf16[2,1024]{1,0:T(2,128)(2,1)S(1)}, u32[]{:S(2)}, u32[]{:S(2)}) collective-permute-start(bf16[2,1024]{1,0:T(2,128)(2,1)S(1)} %get-tuple-element.17), channel_id=1, source_target_pairs={{16,0},{32,16},{48,32},{64,48},{80,64},{96,80},{112,96},{128,112},... | collective-permute-start | bytes 12296 | tf_op jit(solution)/shard_map/ppermute | solution.py:17
  111.3 2.3 copy-start.2
  197.8 6.1 %copy-start.5 = (bf16[5,72,1024]{2,1,0:T(8,128)(2,1)S(1)}, bf16[5,72,1024]{2,1,0:T(8,128)(2,1)}, u32[]{:S(2)}) copy-start(bf16[5,72,1024]{2,1,0:T(8,128)(2,1)} %param.4) | copy-start | bytes 2211844
  197.8 6.1 %collective-permute-start.2 = (bf16[2,72]{0,1:T(8,128)(2,1)S(1)}, bf16[2,72]{0,1:T(8,128)(2,1)S(1)}, u32[]{:S(2)}, u32[]{:S(2)}) collective-permute-start(bf16[2,72]{0,1:T(8,128)(2,1)S(1)} %get-tuple-element.20), channel_id=1, source_target_pairs={{16,0},{32,16},{48,32},{64,48},{80,64},{96,80},{112,96},{128,112},... | collective-permute-start | bytes 872 | tf_op jit(solution)/shard_map/ppermute | solution.py:17
  200.8 4.7 %collective-permute-start.3 = (bf16[2,72]{0,1:T(8,128)(2,1)S(1)}, bf16[2,72]{0,1:T(8,128)(2,1)S(1)}, u32[]{:S(2)}, u32[]{:S(2)}) collective-permute-start(bf16[2,72]{0,1:T(8,128)(2,1)S(1)} %get-tuple-element.21), channel_id=1, source_target_pairs={{0,16},{16,32},{32,48},{48,64},{64,80},{80,96},{96,112},{112,128},... | collective-permute-start | bytes 872 | tf_op jit(solution)/shard_map/ppermute | solution.py:14
  209.1 226.4 %reduce-scatter.5.cloned.1.call-start = ((), (), s32[]{:S(2)}) async-start(), calls=%async_computation.5 | async-start | bytes 2162688 | tf_op jit(solution)/shard_map/reduce_scatter | solution.py:89
  210.7 1.6 copy-start.3
  310.9 126.1 %all-to-all-start = ((bf16[16,2,2048]{2,1,0:T(2,128)(2,1)}), bf16[16,2,2048]{2,1,0:T(2,128)(2,1)S(1)}, u32[]{:S(2)}, u32[]{:S(2)}) async-start(bf16[16,2,2048]{2,1,0:T(2,128)(2,1)} %reshape.40), calls=%async_computation.1 | async-start | bytes 262144 | tf_op jit(solution)/shard_map/all_to_all | solution.py:74
  437.2 1.1 copy-start.1
Sparse Core Ops, SparseCore 0:
  12.2 92.0 all-gather.1
  209.3 99.6 reduce-scatter.2
  313.3 122.1 reduce-scatter.4
where the time goes:
time: 447 us; the launch traced here: 446 us
  waiting for transfers between devices  300 us (67%)
  blocking collectives  81.5 us (18%)
  matrix products  16.3 us (4%)
  starting transfers between devices  15.5 us (3%)
  between operations  14 us (3%)
  local copies, waits for them, and re-layouts  11.2 us (3%)
  other arithmetic  7.52 us (2%)
    reduce_scatter x1, waiting for transfers between devices, per_device(): lax.psum_scatter(jnp.stack(pieces, axis=1).astype(jnp.bfloat16), 'seq', s...  115 us
    reduce_scatter x1, waiting for transfers between devices, per_device(): lax.psum_scatter(running.astype(jnp.bfloat16), 'sub', scatter_dimension=1...  92.8 us
    all_gather x1, waiting for transfers between devices, per_device(): gathered = lax.all_gather(pooled, 'sub', axis=0, tiled=True)  91.6 us
    psum x1, blocking collectives, per_device(): lax.psum(jnp.sum(slope_second * normed_second, axis=1), 'sub')  42.8 us
    psum x1, blocking collectives, per_device(): square_sum = lax.psum(jnp.sum(y_float * y_float, axis=1), 'sub')  38.7 us
  transfers between devices with their start and end apart: 8, of which 4 were waited for; matrix products, arithmetic and copies ran while one was open for 4% of the time, Pallas kernels for 0%

commit v1 on v0

--- a/solution.py
+++ b/solution.py
@@ -40,7 +40,8 @@
     inv_first = lax.rsqrt(jnp.mean(x_float * x_float, axis=1, keepdims=True) + EPSILON)
     normed_first = x_float * inv_first
     pooled = pool_pairs(jax.nn.gelu(normed_first, approximate=False)).astype(jnp.bfloat16)
-    gathered = lax.all_gather(pooled, "sub", axis=0, tiled=True)
+    repeated = jnp.stack([pooled] * lax.axis_size("sub"))
+    gathered = jnp.concatenate(lax.all_to_all(repeated, "sub", 0, 0), axis=0)
     block_rows = gathered.shape[0]
     padded = padded_2(gathered, (("seq", 0),), 2)
     conv_acc = jnp.zeros((block_rows, out_width), jnp.float32)

time: 447 us -> 412 us (0.922)
  waiting for transfers between devices: 300 us -> 253 us
  starting transfers between devices: 15.5 us -> 24.8 us
  blocking collectives: 81.5 us -> 86.1 us
    all_gather x1 -> x0, waiting for transfers between devices: 91.6 us -> none  [per_device(): gathered = lax.all_gather(pooled, 'sub', axis=0, tiled=True)]
    all_to_all x0 -> x1, waiting for transfers between devices: none -> 40.4 us  [per_device(): gathered = jnp.concatenate(lax.all_to_all(repeated, 'sub', 0, 0), axis=0)]
    all_to_all x0 -> x1, starting transfers between devices: none -> 9.43 us  [per_device(): gathered = jnp.concatenate(lax.all_to_all(repeated, 'sub', 0, 0), axis=0)]
    psum x1, blocking collectives: 38.7 us -> 43.2 us  [per_device(): square_sum = lax.psum(jnp.sum(y_float * y_float, axis=1), 'sub')]
where the time goes in v1:
time: 412 us; the launch traced here: 411 us
  waiting for transfers between devices  253 us (61%)
  blocking collectives  86.1 us (21%)
  starting transfers between devices  24.8 us (6%)
  matrix products  15.7 us (4%)
  between operations  14.3 us (3%)
  local copies, waits for them, and re-layouts  10.6 us (3%)
  other arithmetic  6.85 us (2%)
    reduce_scatter x1, waiting for transfers between devices, per_device(): lax.psum_scatter(jnp.stack(pieces, axis=1).astype(jnp.bfloat16), 'seq', s...  115 us
    reduce_scatter x1, waiting for transfers between devices, per_device(): lax.psum_scatter(running.astype(jnp.bfloat16), 'sub', scatter_dimension=1...  95.8 us
    psum x1, blocking collectives, per_device(): square_sum = lax.psum(jnp.sum(y_float * y_float, axis=1), 'sub')  43.2 us
    psum x1, blocking collectives, per_device(): lax.psum(jnp.sum(slope_second * normed_second, axis=1), 'sub')  42.9 us
    all_to_all x1, waiting for transfers between devices, per_device(): gathered = jnp.concatenate(lax.all_to_all(repeated, 'sub', 0, 0), axis=0)  40.4 us
    all_to_all x1, starting transfers between devices, per_device(): gathered = jnp.concatenate(lax.all_to_all(repeated, 'sub', 0, 0), axis=0)  9.43 us
  transfers between devices with their start and end apart: 8, of which 4 were waited for; matrix products, arithmetic and copies ran while one was open for 4% of the time, Pallas kernels for 0%

profile of v1, /device:TPU:8, one launch (start us, length us, event | category | flops | bytes accessed | tf_op | source)
XLA Modules:
  0.0 411.4 jit_solution(12284457120379499315)
XLA Ops:
  7.2 1.1 fusion.66
  8.3 2.2 fusion.28
  10.4 0.3 reshape.43
  10.7 0.6 reduce_sum.55
  11.4 1.6 stack.20
  13.0 9.4 %all-to-all-start = ((bf16[16,64,1024]{2,1,0:T(8,128)(2,1)}), bf16[16,64,1024]{2,1,0:T(8,128)(2,1)S(1)}, u32[]{:S(2)}, u32[]{:S(2)}) async-start(bf16[16,64,1024]{2,1,0:T(8,128)(2,1)} %stack.20), calls=%async_computation | async-start | bytes 4194304 | tf_op jit(solution)/shard_map/all_to_all | solution.py:44
  22.6 0.2 broadcast_in_dim.4
  22.8 0.2 copy.14
  23.0 40.4 %all-to-all-done = bf16[16,64,1024]{2,1,0:T(8,128)(2,1)S(1)} async-done(((bf16[16,64,1024]{2,1,0:T(8,128)(2,1)}), bf16[16,64,1024]{2,1,0:T(8,128)(2,1)S(1)}, u32[]{:S(2)}, u32[]{:S(2)}) %all-to-all-start) | async-done | bytes 2097184 | tf_op jit(solution)/shard_map/all_to_all | solution.py:44
  63.4 1.3 collective-permute-start
  64.7 1.3 collective-permute-start.1
  66.0 1.7 fusion.98
  67.7 1.8 collective-permute-done.1
  69.5 0.8 fusion.4
  70.3 0.7 fusion.2
  71.0 0.8 fusion.7
  71.8 1.7 multiply_reduce_fusion.1
  73.5 43.2 %psum.14 = f32[1024]{0:T(1024)S(1)} all-reduce(f32[1024]{0:T(1024)S(1)} %get-tuple-element.22), channel_id=1, replica_groups=mesh['seq'=32,'sub'=16] {'sub'}, use_global_device_ids=true, to_apply=%region_3.0 | all-reduce | flops 1024 | bytes 8192 | tf_op jit(solution)/shard_map/psum | solution.py:57
  116.9 42.9 %psum.15 = f32[1024]{0:T(1024)S(1)} all-reduce(f32[1024]{0:T(1024)S(1)} %get-tuple-element.14), channel_id=1, replica_groups=mesh['seq'=32,'sub'=16] {'sub'}, use_global_device_ids=true, to_apply=%region_6.0 | all-reduce | flops 1024 | bytes 8192 | tf_op jit(solution)/shard_map/psum | solution.py:63
  159.8 0.7 multiply_convert_fusion
  160.6 1.4 collective-permute-start.2
  162.0 1.7 fusion.96
  163.6 3.0 collective-permute-start.3
  166.7 0.8 fusion.90
  167.5 0.8 fusion.86
  168.3 0.8 fusion.83
  169.1 2.8 add_convert_fusion
  171.9 0.2 reduce-scatter.5.cloned.1.call-start
  172.2 0.7 fusion.13
  172.8 0.7 fusion.19
  173.5 0.5 fusion.15
  174.0 0.7 fusion.17
  174.7 0.7 fusion.21
  175.4 2.5 copy.17
  177.9 95.8 %reduce-scatter.3.cloned.1.call-done = bf16[1024,64]{0,1:T(8,128)(2,1)} async-done(((bf16[1024,1024]{0,1:T(8,128)(2,1)}), bf16[1024,64]{0,1:T(8,128)(2,1)}) %reduce-scatter.3.cloned.1.call-update) | async-done | bytes 131088 | tf_op jit(solution)/shard_map/reduce_scatter | solution.py:72
  273.6 1.1 copy.20
  274.7 0.9 reshape.46
  275.6 8.1 %all-to-all-start.1 = ((bf16[16,2,2048]{2,1,0:T(2,128)(2,1)}), bf16[16,2,2048]{2,1,0:T(2,128)(2,1)S(1)}, u32[]{:S(2)}, u32[]{:S(2)}) async-start(bf16[16,2,2048]{2,1,0:T(2,128)(2,1)} %reshape.46), calls=%async_computation.2 | async-start | bytes 262144 | tf_op jit(solution)/shard_map/all_to_all | solution.py:75
  283.7 0.2 copy.12
  283.9 0.6 reduce_sum.57
  284.6 0.7 copy.18
  285.3 115.1 %reduce-scatter.5.cloned.1.call-done = bf16[32,5,72]{2,1,0:T(8,128)(2,1)} async-done(((bf16[1024,5,72]{2,1,0:T(8,128)(2,1)}), bf16[32,5,72]{2,1,0:T(8,128)(2,1)}) %reduce-scatter.5.cloned.1.call-update) | async-done | bytes 23056 | tf_op jit(solution)/shard_map/reduce_scatter | solution.py:90
  400.4 1.5 copy.19
  401.9 0.2 reshape.47
  402.2 0.3 copy.16
  402.8 0.4 mul.196
  403.2 0.4 fusion.65
  403.6 0.9 fusion.63
  (29 shorter events, 1.0 us)
Async XLA Ops:
  13.0 9.5 %copy-start.3 = (bf16[512,72]{0,1:T(8,128)(2,1)S(1)}, bf16[512,72]{0,1:T(8,128)(2,1)}, u32[]{:S(2)}) copy-start(bf16[512,72]{0,1:T(8,128)(2,1)} %param.5) | copy-start | bytes 221188
  13.0 50.4 %all-to-all-start = ((bf16[16,64,1024]{2,1,0:T(8,128)(2,1)}), bf16[16,64,1024]{2,1,0:T(8,128)(2,1)S(1)}, u32[]{:S(2)}, u32[]{:S(2)}) async-start(bf16[16,64,1024]{2,1,0:T(8,128)(2,1)} %stack.20), calls=%async_computation | async-start | bytes 4194304 | tf_op jit(solution)/shard_map/all_to_all | solution.py:44
  22.4 251.2 %reduce-scatter.3.cloned.1.call-start = ((), (), s32[]{:S(2)}) async-start(), calls=%async_computation.4 | async-start | bytes 2228224 | tf_op jit(solution)/shard_map/reduce_scatter | solution.py:72
  23.0 46.5 %copy-start.1 = (bf16[5,72,1024]{2,1,0:T(8,128)(2,1)S(1)}, bf16[5,72,1024]{2,1,0:T(8,128)(2,1)}, u32[]{:S(2)}) copy-start(bf16[5,72,1024]{2,1,0:T(8,128)(2,1)} %param.4) | copy-start | bytes 2211844
  63.4 6.9 %collective-permute-start = (bf16[2,1024]{1,0:T(2,128)(2,1)S(1)}, bf16[2,1024]{1,0:T(2,128)(2,1)S(1)}, u32[]{:S(2)}, u32[]{:S(2)}) collective-permute-start(bf16[2,1024]{1,0:T(2,128)(2,1)S(1)} %get-tuple-element.16), channel_id=1, source_target_pairs={{0,16},{16,32},{32,48},{48,64},{64,80},{80,96},{96,112},{112,128},... | collective-permute-start | bytes 12296 | tf_op jit(solution)/shard_map/ppermute | solution.py:14
  64.7 4.8 %collective-permute-start.1 = (bf16[2,1024]{1,0:T(2,128)(2,1)S(1)}, bf16[2,1024]{1,0:T(2,128)(2,1)S(1)}, u32[]{:S(2)}, u32[]{:S(2)}) collective-permute-start(bf16[2,1024]{1,0:T(2,128)(2,1)S(1)} %get-tuple-element.17), channel_id=1, source_target_pairs={{16,0},{32,16},{48,32},{64,48},{80,64},{96,80},{112,96},{128,112},... | collective-permute-start | bytes 12296 | tf_op jit(solution)/shard_map/ppermute | solution.py:17
  160.6 6.1 %copy-start.2 = (bf16[5,72,1024]{2,1,0:T(8,128)(2,1)S(1)}, bf16[5,72,1024]{2,1,0:T(8,128)(2,1)}, u32[]{:S(2)}) copy-start(bf16[5,72,1024]{2,1,0:T(8,128)(2,1)} %param.4) | copy-start | bytes 2211844
  160.6 6.1 %collective-permute-start.2 = (bf16[2,72]{0,1:T(8,128)(2,1)S(1)}, bf16[2,72]{0,1:T(8,128)(2,1)S(1)}, u32[]{:S(2)}, u32[]{:S(2)}) collective-permute-start(bf16[2,72]{0,1:T(8,128)(2,1)S(1)} %get-tuple-element.20), channel_id=1, source_target_pairs={{16,0},{32,16},{48,32},{64,48},{80,64},{96,80},{112,96},{128,112},... | collective-permute-start | bytes 872 | tf_op jit(solution)/shard_map/ppermute | solution.py:17
  163.6 4.7 %collective-permute-start.3 = (bf16[2,72]{0,1:T(8,128)(2,1)S(1)}, bf16[2,72]{0,1:T(8,128)(2,1)S(1)}, u32[]{:S(2)}, u32[]{:S(2)}) collective-permute-start(bf16[2,72]{0,1:T(8,128)(2,1)S(1)} %get-tuple-element.21), channel_id=1, source_target_pairs={{0,16},{16,32},{32,48},{48,64},{64,80},{80,96},{96,112},{112,128},... | collective-permute-start | bytes 872 | tf_op jit(solution)/shard_map/ppermute | solution.py:14
  171.9 228.5 %reduce-scatter.5.cloned.1.call-start = ((), (), s32[]{:S(2)}) async-start(), calls=%async_computation.5 | async-start | bytes 2162688 | tf_op jit(solution)/shard_map/reduce_scatter | solution.py:90
  275.6 126.3 %all-to-all-start.1 = ((bf16[16,2,2048]{2,1,0:T(2,128)(2,1)}), bf16[16,2,2048]{2,1,0:T(2,128)(2,1)S(1)}, u32[]{:S(2)}, u32[]{:S(2)}) async-start(bf16[16,2,2048]{2,1,0:T(2,128)(2,1)} %reshape.46), calls=%async_computation.2 | async-start | bytes 262144 | tf_op jit(solution)/shard_map/all_to_all | solution.py:75
  402.1 1.1 copy-start
Sparse Core Ops, SparseCore 0:
  172.1 101.5 reduce-scatter.2
  278.0 122.3 reduce-scatter.4
